TPU v7x, 32 devices: a whole 2x2x4 slice. The times are simulated.
32 devices in a mesh: gx: 4 (over x, core), gy: 8 (over z, y).
Axes of the slice: x: 2, y: 2, z: 4, core: 2. Of those that a mesh axis runs over, the one named last changes fastest.
Arguments:
- first_image: float32 [32, 64, 128], P('gx', 'gy'), may hold values from -6 to 6
- second_image: float32 [32, 64, 128], P('gx', 'gy'), may hold values from -6 to 6
- start_flow: float32 [3, 32, 64, 128], P(None, 'gx', 'gy'), may hold values from -3 to 3
Outputs:
- flow: float32 [3, 32, 64, 128], P(None, 'gx', 'gy')
All inputs are finite; a program needn't handle non-finite values.
Results may differ from a plain program's by a relative error of at most 0.0001.
Values sent between devices are 32-bit elements; how exact they have to be, the bound alone decides.
A program may use at most 128 MiB of HBM per device.

v0:
```python
import jax
import jax.numpy as jnp
from jax import lax
from jax.sharding import PartitionSpec as P

SWEEPS = 4
COARSE_SWEEPS = 12
CYCLES = 2


damping = 0.6
smooth_weight = 2.0
edge_scale = 0.25
floor_grad = 0.5


def extended(cells, sides, width):
    for axis, dim in sides:
        count = lax.axis_size(axis)
        ends = count - 1
        head = lax.slice_in_dim(cells, 0, width, axis=dim)
        tail = lax.slice_in_dim(cells, cells.shape[dim] - width, cells.shape[dim], axis=dim)
        cells = jnp.concatenate(
            [
                lax.ppermute(tail, axis, [(i, (i + 1) % count) for i in range(ends)]),
                cells,
                lax.ppermute(head, axis, [((i + 1) % count, i) for i in range(ends)]),
            ],
            axis=dim,
        )
    return cells


def pad_depth(field):
    widths = [(0, 0)] * (field.ndim - 1) + [(1, 1)]
    return jnp.pad(field, widths)


def pad_cells(field):
    widths = [(0, 0)] * (field.ndim - 3) + [(1, 1)] * 3
    return jnp.pad(field, widths)


def neighbours(padded):
    return [
        padded[..., 2:, 1:-1, 1:-1],
        padded[..., :-2, 1:-1, 1:-1],
        padded[..., 1:-1, 2:, 1:-1],
        padded[..., 1:-1, :-2, 1:-1],
        padded[..., 1:-1, 1:-1, 2:],
        padded[..., 1:-1, 1:-1, :-2],
    ]


def centre(padded):
    return padded[..., 1:-1, 1:-1, 1:-1]


def diffusivity(padded_flow):
    beside_all = neighbours(padded_flow)
    total = jnp.zeros(centre(padded_flow).shape[1:], padded_flow.dtype)
    for upper, lower in ((0, 1), (2, 3), (4, 5)):
        slope = 0.5 * (beside_all[upper] - beside_all[lower])
        total = total + jnp.sum(slope * slope, axis=0)
    return lax.rsqrt(1.0 + total / edge_scale)


def motion_tensor(padded_images):
    mean_image = 0.5 * (padded_images[0] + padded_images[1])
    beside_all = neighbours(mean_image)
    slopes = [
        0.5 * (beside_all[0] - beside_all[1]),
        0.5 * (beside_all[2] - beside_all[3]),
        0.5 * (beside_all[4] - beside_all[5]),
    ]
    change = centre(padded_images[1]) - centre(padded_images[0])
    scale = 1.0 / (
        slopes[0] * slopes[0] + slopes[1] * slopes[1] + slopes[2] * slopes[2] + floor_grad
    )
    tensor = jnp.stack(
        [
            scale * slopes[0] * slopes[0],
            scale * slopes[0] * slopes[1],
            scale * slopes[0] * slopes[2],
            scale * slopes[1] * slopes[1],
            scale * slopes[1] * slopes[2],
            scale * slopes[2] * slopes[2],
        ]
    )
    source = jnp.stack(
        [-scale * slopes[0] * change, -scale * slopes[1] * change, -scale * slopes[2] * change]
    )
    return (tensor, source)


def apply_sym(matrix, vector):
    first = matrix[0] * vector[0] + matrix[1] * vector[1] + matrix[2] * vector[2]
    second = matrix[1] * vector[0] + matrix[3] * vector[1] + matrix[4] * vector[2]
    third = matrix[2] * vector[0] + matrix[4] * vector[1] + matrix[5] * vector[2]
    return jnp.stack([first, second, third])


def inverse_sym(tensor, total):
    aaa = tensor[0] + total
    bbb = tensor[1]
    ccc = tensor[2]
    ddd = tensor[3] + total
    eee = tensor[4]
    fff = tensor[5] + total
    cof_a = ddd * fff - eee * eee
    cof_b = ccc * eee - bbb * fff
    cof_c = bbb * eee - ccc * ddd
    cof_d = aaa * fff - ccc * ccc
    cof_e = bbb * ccc - aaa * eee
    cof_f = aaa * ddd - bbb * bbb
    determinant = aaa * cof_a + bbb * cof_b + ccc * cof_c
    return jnp.stack([cof_a, cof_b, cof_c, cof_d, cof_e, cof_f]) / determinant


def prepare(tensor, padded_weight, scale):
    middle = centre(padded_weight)
    faces = [scale * 2.0 * middle * other / (middle + other) for other in neighbours(padded_weight)]
    total = faces[0] + faces[1] + faces[2] + faces[3] + faces[4] + faces[5]
    return (tensor, jnp.stack(faces), total, inverse_sym(tensor, total))


def inflow(padded_field, level):
    faces = level[1]
    beside_all = neighbours(padded_field)
    result = faces[0] * beside_all[0]
    for index in range(1, 6):
        result = result + faces[index] * beside_all[index]
    return result


def relaxed(field, padded_field, source, level):
    return (1.0 - damping) * field + damping * apply_sym(
        level[3], source + inflow(padded_field, level)
    )


def residual(field, padded_field, source, level):
    return source + inflow(padded_field, level) - apply_sym(level[0], field) - level[2] * field


def restrict(field, ratio):
    front = field.shape[:-3]
    across, along, depth = field.shape[-3:]
    blocks = field.reshape(
        front + (across // ratio, ratio, along // ratio, ratio, depth // ratio, ratio)
    )
    return jnp.mean(blocks, axis=(-5, -3, -1))


def refine(padded, axis, ratio):
    count = padded.shape[axis] - 2
    middle = lax.slice_in_dim(padded, 1, count + 1, axis=axis)
    below = lax.slice_in_dim(padded, 0, count, axis=axis)
    above = lax.slice_in_dim(padded, 2, count + 2, axis=axis)
    pieces = []
    for offset in range(ratio):
        shift = (offset + 0.5) / ratio - 0.5
        other = below if shift < 0 else above
        pieces.append((1.0 - abs(shift)) * middle + abs(shift) * other)
    stacked = jnp.stack(pieces, axis=axis + 1)
    shape = list(middle.shape)
    shape[axis] = count * ratio
    return stacked.reshape(shape)


def refine_cells(padded, ratio):
    for axis in (1, 2, 3):
        padded = refine(padded, axis, ratio)
    return padded


def fine_pad(field):
    return pad_depth(extended(field, (("gx", 1), ("gy", 2)), 1))


def mid_pad(field):
    return pad_depth(extended(field, (("gx", 1), ("gy", 2)), 1))


def coarse_relax(source, level, padder):
    correction = damping * apply_sym(level[3], source)

    def coarse_turn(index, current):
        return relaxed(current, padder(current), source, level)

    return lax.fori_loop(0, COARSE_SWEEPS - 1, coarse_turn, correction)


def body(first_image, second_image, start_flow):
    images = jnp.stack([first_image, second_image])
    padded_images = pad_depth(extended(images, (("gx", 1), ("gy", 2)), 1))
    tensor, source = motion_tensor(padded_images)
    mid_tensor = restrict(tensor, 2)
    coarse_tensor = restrict(mid_tensor, 4)
    flow = start_flow
    for cycle in range(CYCLES):
        padded = fine_pad(flow)
        weight = diffusivity(padded)
        padded_weight = pad_depth(extended(weight, (("gx", 0), ("gy", 1)), 1))
        fine = prepare(tensor, padded_weight, smooth_weight)
        flow = relaxed(flow, padded, source, fine)
        for sweep in range(SWEEPS - 1):
            flow = relaxed(flow, fine_pad(flow), source, fine)
        fine_rest = residual(flow, fine_pad(flow), source, fine)
        mid_weight = restrict(weight, 2)
        padded_mid = pad_depth(extended(mid_weight, (("gx", 0), ("gy", 1)), 1))
        mid = prepare(mid_tensor, padded_mid, smooth_weight / 4.0)
        mid_source = restrict(fine_rest, 2)
        error = damping * apply_sym(mid[3], mid_source)
        for sweep in range(SWEEPS - 1):
            error = relaxed(error, mid_pad(error), mid_source, mid)
        mid_rest = residual(error, mid_pad(error), mid_source, mid)
        coarse_source = restrict(mid_rest, 4)
        bundle = jnp.concatenate([coarse_tensor, coarse_source])
        rows = lax.axis_size("gx")
        cols = lax.axis_size("gy")
        coarse_x, coarse_y, depth = bundle.shape[1:]
        whole = lax.all_gather(bundle[None], ("gx", "gy"), axis=0, tiled=True)
        whole = whole.reshape((rows, cols) + bundle.shape).transpose(2, 0, 3, 1, 4, 5)
        whole = whole.reshape(9, rows * coarse_x, cols * coarse_y, depth)
        unit_weight = jnp.ones(whole.shape[1:], jnp.float32)
        coarse = prepare(whole[:6], pad_cells(unit_weight), smooth_weight / 64.0)
        correction = coarse_relax(whole[6:], coarse, pad_cells)
        start_x = lax.axis_index("gx") * coarse_x
        start_y = lax.axis_index("gy") * coarse_y
        lifted = lax.dynamic_slice(
            pad_cells(correction),
            (0, start_x, start_y, 0),
            (3, coarse_x + 2, coarse_y + 2, depth + 2),
        )
        error = error + refine_cells(lifted, 4)
        for sweep in range(SWEEPS):
            error = relaxed(error, mid_pad(error), mid_source, mid)
        raised = pad_depth(extended(error, (("gx", 1), ("gy", 2)), 1))
        flow = flow + refine_cells(raised, 2)
        for sweep in range(SWEEPS):
            flow = relaxed(flow, fine_pad(flow), source, fine)
    return flow


def solution(mesh):
    return jax.shard_map(
        body,
        mesh=mesh,
        in_specs=(P("gx", "gy", None), P("gx", "gy", None), P(None, "gx", "gy", None)),
        out_specs=P(None, "gx", "gy", None),
        check_vma=False,
    )
```

profile of v0, /device:TPU:0, one launch (start us, length us, event | category | flops | bytes accessed | tf_op | source)
XLA Modules:
  0.0 849.8 jit_solution(11091146432861596911)
XLA Ops:
  7.1 5.1 collective-permute-start.5
  21.5 5.0 collective-permute-start.7
  42.0 5.4 collective-permute-start.27
  48.8 5.9 collective-permute-start.11
  93.9 5.2 collective-permute-start.15
  107.9 5.6 collective-permute-start.19
  117.0 4.8 collective-permute-start.21
  124.0 5.7 collective-permute-start.23
  133.1 4.8 collective-permute-start.29
  140.0 5.7 collective-permute-start.31
  147.7 7.6 reshape.215
  160.0 4.8 collective-permute-start.33
  167.0 5.7 collective-permute-start.35
  175.7 4.8 collective-permute-start.37
  182.6 5.7 collective-permute-start.39
  191.3 4.8 collective-permute-start.41
  198.2 5.7 collective-permute-start.43
  213.8 5.7 collective-permute-start.47
  221.4 75.0 %all-gather = f32[288,1,1,16]{3,2,1,0:T(1,128)S(1)} all-gather(f32[9,1,1,16]{3,2,1,0:T(1,128)S(1)} %copy.3445), channel_id=2, replica_groups=mesh['gx'=4,'gy'=8] {'gx','gy'}, dimensions={0}, use_global_device_ids=true | all-gather | bytes 19008 | tf_op jit(solution)/shard_map/all_gather | solution.py:223
  325.9 4.8 collective-permute-start.55
  340.1 5.2 collective-permute-start.59
  348.2 5.0 collective-permute-start.61
  355.4 5.7 collective-permute-start.63
  371.0 5.9 collective-permute-start.66
  381.2 4.8 collective-permute-start.69
  388.2 5.7 collective-permute-start.71
  397.1 4.8 collective-permute-start.73
  404.1 5.7 collective-permute-start.75
  413.1 4.8 collective-permute-start.77
  420.0 5.7 collective-permute-start.79
  429.0 4.8 collective-permute-start.81
  436.0 5.7 collective-permute-start.83
  445.0 4.8 collective-permute-start.85
  452.0 5.7 collective-permute-start.87
  473.9 5.7 collective-permute-start.107
  487.6 5.7 collective-permute-start.91
  503.2 5.2 collective-permute-start.95
  511.7 5.1 collective-permute-start.97
  519.0 5.7 collective-permute-start.99
  528.0 4.8 collective-permute-start.101
  535.0 5.7 collective-permute-start.103
  544.1 4.8 collective-permute-start.109
  551.1 6.0 collective-permute-start.111
  558.7 7.6 reshape.223
  571.0 4.8 collective-permute-start.113
  577.9 5.7 collective-permute-start.115
  586.6 4.8 collective-permute-start.117
  593.5 5.7 collective-permute-start.119
  609.1 5.7 collective-permute-start.123
  624.7 5.7 collective-permute-start.127
  632.3 75.0 %all-gather.1 = f32[288,1,1,16]{3,2,1,0:T(1,128)S(1)} all-gather(f32[9,1,1,16]{3,2,1,0:T(1,128)S(1)} %copy.3475), channel_id=3, replica_groups=mesh['gx'=4,'gy'=8] {'gx','gy'}, dimensions={0}, use_global_device_ids=true | all-gather | bytes 19008 | tf_op jit(solution)/shard_map/all_gather | solution.py:223
  731.0 4.8 collective-permute-start.135
  745.1 5.2 collective-permute-start.139
  753.2 5.0 collective-permute-start.141
  760.4 5.7 collective-permute-start.143
  776.0 5.7 collective-permute-start.146
  786.3 4.8 collective-permute-start.149
  793.2 5.7 collective-permute-start.151
  802.2 4.8 collective-permute-start.153
  809.1 5.7 collective-permute-start.155
  818.1 4.8 collective-permute-start.157
  825.1 5.7 collective-permute-start.159
  834.1 4.8 collective-permute-start.161
  841.0 5.7 collective-permute-start.163
  (945 shorter events, 361.8 us)
Async XLA Ops:
  0.7 11.5 %collective-permute-start.1 = (f32[2,1,8,128]{3,2,1,0:T(8,128)S(1)}, f32[2,1,8,128]{3,2,1,0:T(8,128)S(1)}, u32[]{:S(2)}, u32[]{:S(2)}) collective-permute-start(f32[2,1,8,128]{3,2,1,0:T(8,128)S(1)} %get-tuple-element.835), channel_id=1, source_target_pairs={{8,0},{16,8},{24,16},{9,1},{17,9},{25,17},{10,2},{18,10},{26,18},{... | collective-permute-start | bytes 24584 | tf_op jit(solution)/shard_map/ppermute | solution.py:27
  2.0 10.2 %collective-permute-start = (f32[2,1,8,128]{3,2,1,0:T(8,128)S(1)}, f32[2,1,8,128]{3,2,1,0:T(8,128)S(1)}, u32[]{:S(2)}, u32[]{:S(2)}) collective-permute-start(f32[2,1,8,128]{3,2,1,0:T(8,128)S(1)} %get-tuple-element.834), channel_id=1, source_target_pairs={{0,8},{8,16},{16,24},{1,9},{9,17},{17,25},{2,10},{10,18},{18,26},{... | collective-permute-start | bytes 24584 | tf_op jit(solution)/shard_map/ppermute | solution.py:25
  5.8 13.2 %collective-permute-start.4 = (f32[3,1,8,128]{3,2,1,0:T(8,128)S(1)}, f32[3,1,8,128]{3,2,1,0:T(8,128)S(1)}, u32[]{:S(2)}, u32[]{:S(2)}) collective-permute-start(f32[3,1,8,128]{3,2,1,0:T(8,128)S(1)} %get-tuple-element.768), channel_id=1, source_target_pairs={{8,0},{16,8},{24,16},{9,1},{17,9},{25,17},{10,2},{18,10},{26,18},{... | collective-permute-start | bytes 36872 | tf_op jit(solution)/shard_map/ppermute | solution.py:27
  7.1 11.9 %collective-permute-start.5 = (f32[3,1,8,128]{3,2,1,0:T(8,128)S(1)}, f32[3,1,8,128]{3,2,1,0:T(8,128)S(1)}, u32[]{:S(2)}, u32[]{:S(2)}) collective-permute-start(f32[3,1,8,128]{3,2,1,0:T(8,128)S(1)} %get-tuple-element.769), channel_id=1, source_target_pairs={{0,8},{8,16},{16,24},{1,9},{9,17},{17,25},{2,10},{10,18},{18,26},{... | collective-permute-start | bytes 36872 | tf_op jit(solution)/shard_map/ppermute | solution.py:25
  13.1 13.3 %collective-permute-start.3 = (f32[2,10,1,128]{3,0,2,1:T(2,128)S(1)}, f32[2,10,1,128]{3,0,2,1:T(2,128)S(1)}, u32[]{:S(2)}, u32[]{:S(2)}) collective-permute-start(f32[2,10,1,128]{3,0,2,1:T(2,128)S(1)} %copy.3495), channel_id=1, source_target_pairs={{1,0},{2,1},{3,2},{4,3},{5,4},{6,5},{7,6},{9,8},{10,9},{11,10},{12... | collective-permute-start | bytes 30728 | tf_op jit(solution)/shard_map/ppermute | solution.py:27
  14.5 12.0 %collective-permute-start.2 = (f32[2,10,1,128]{3,0,2,1:T(2,128)S(1)}, f32[2,10,1,128]{3,0,2,1:T(2,128)S(1)}, u32[]{:S(2)}, u32[]{:S(2)}) collective-permute-start(f32[2,10,1,128]{3,0,2,1:T(2,128)S(1)} %copy.3494), channel_id=1, source_target_pairs={{0,1},{1,2},{2,3},{3,4},{4,5},{5,6},{6,7},{8,9},{9,10},{10,11},{11... | collective-permute-start | bytes 30728 | tf_op jit(solution)/shard_map/ppermute | solution.py:25
  20.2 8.1 collective-permute-start.6
  31.2 9.4 %collective-permute-start.25 = (f32[1,4,64]{2,1,0:T(4,128)S(1)}, f32[1,4,64]{2,1,0:T(4,128)S(1)}, u32[]{:S(2)}, u32[]{:S(2)}) collective-permute-start(f32[1,4,64]{2,1,0:T(4,128)S(1)} %get-tuple-element.958), channel_id=1, source_target_pairs={{0,8},{8,16},{16,24},{1,9},{9,17},{17,25},{2,10},{10,18},{18,26},{... | collective-permute-start | bytes 3080 | tf_op jit(solution)/shard_map/ppermute | solution.py:25
  35.3 12.1 %collective-permute-start.8 = (f32[1,8,128]{2,1,0:T(8,128)S(1)}, f32[1,8,128]{2,1,0:T(8,128)S(1)}, u32[]{:S(2)}, u32[]{:S(2)}) collective-permute-start(f32[1,8,128]{2,1,0:T(8,128)S(1)} %get-tuple-element.887), channel_id=1, source_target_pairs={{8,0},{16,8},{24,16},{9,1},{17,9},{25,17},{10,2},{18,10},{26,18},{... | collective-permute-start | bytes 12296 | tf_op jit(solution)/shard_map/ppermute | solution.py:27
  36.6 10.9 %collective-permute-start.9 = (f32[1,8,128]{2,1,0:T(8,128)S(1)}, f32[1,8,128]{2,1,0:T(8,128)S(1)}, u32[]{:S(2)}, u32[]{:S(2)}) collective-permute-start(f32[1,8,128]{2,1,0:T(8,128)S(1)} %get-tuple-element.886), channel_id=1, source_target_pairs={{0,8},{8,16},{16,24},{1,9},{9,17},{17,25},{2,10},{10,18},{18,26},{... | collective-permute-start | bytes 12296 | tf_op jit(solution)/shard_map/ppermute | solution.py:25
  40.7 14.0 %collective-permute-start.26 = (f32[6,1,64]{2,1,0:T(1,128)S(1)}, f32[6,1,64]{2,1,0:T(1,128)S(1)}, u32[]{:S(2)}, u32[]{:S(2)}) collective-permute-start(f32[6,1,64]{2,1,0:T(1,128)S(1)} %get-tuple-element.954), channel_id=1, source_target_pairs={{1,0},{2,1},{3,2},{4,3},{5,4},{6,5},{7,6},{9,8},{10,9},{11,10},{12... | collective-permute-start | bytes 4616 | tf_op jit(solution)/shard_map/ppermute | solution.py:27
  42.0 12.7 %collective-permute-start.27 = (f32[6,1,64]{2,1,0:T(1,128)S(1)}, f32[6,1,64]{2,1,0:T(1,128)S(1)}, u32[]{:S(2)}, u32[]{:S(2)}) collective-permute-start(f32[6,1,64]{2,1,0:T(1,128)S(1)} %get-tuple-element.953), channel_id=1, source_target_pairs={{0,1},{1,2},{2,3},{3,4},{4,5},{5,6},{6,7},{8,9},{9,10},{10,11},{11... | collective-permute-start | bytes 4616 | tf_op jit(solution)/shard_map/ppermute | solution.py:25
  47.5 8.0 collective-permute-start.10
  107.9 7.0 collective-permute-start.19
  122.7 7.1 collective-permute-start.22
  124.0 7.1 collective-permute-start.23
  138.7 7.1 collective-permute-start.30
  140.0 7.1 collective-permute-start.31
  165.7 7.0 collective-permute-start.34
  167.0 7.1 collective-permute-start.35
  181.3 7.0 collective-permute-start.38
  182.6 7.1 collective-permute-start.39
  196.9 7.2 collective-permute-start.42
  198.2 7.1 collective-permute-start.43
  212.5 7.1 collective-permute-start.46
  213.8 7.1 collective-permute-start.47
  354.1 7.0 collective-permute-start.62
  355.4 7.1 collective-permute-start.63
  369.7 7.2 collective-permute-start.67
  371.0 7.1 collective-permute-start.66
  386.9 7.0 collective-permute-start.70
  388.2 7.1 collective-permute-start.71
  404.1 7.1 collective-permute-start.75
  418.7 7.0 collective-permute-start.78
  420.0 7.1 collective-permute-start.79
  434.7 7.0 collective-permute-start.82
  436.0 7.1 collective-permute-start.83
  450.7 7.0 collective-permute-start.86
  452.0 7.1 collective-permute-start.87
  472.6 13.0 %collective-permute-start.106 = (f32[6,1,64]{2,1,0:T(1,128)S(1)}, f32[6,1,64]{2,1,0:T(1,128)S(1)}, u32[]{:S(2)}, u32[]{:S(2)}) collective-permute-start(f32[6,1,64]{2,1,0:T(1,128)S(1)} %get-tuple-element.952), channel_id=1, source_target_pairs={{1,0},{2,1},{3,2},{4,3},{5,4},{6,5},{7,6},{9,8},{10,9},{11,10},{12... | collective-permute-start | bytes 4616 | tf_op jit(solution)/shard_map/ppermute | solution.py:27
  473.9 11.7 %collective-permute-start.107 = (f32[6,1,64]{2,1,0:T(1,128)S(1)}, f32[6,1,64]{2,1,0:T(1,128)S(1)}, u32[]{:S(2)}, u32[]{:S(2)}) collective-permute-start(f32[6,1,64]{2,1,0:T(1,128)S(1)} %get-tuple-element.951), channel_id=1, source_target_pairs={{0,1},{1,2},{2,3},{3,4},{4,5},{5,6},{6,7},{8,9},{9,10},{10,11},{11... | collective-permute-start | bytes 4616 | tf_op jit(solution)/shard_map/ppermute | solution.py:25
  486.3 7.1 collective-permute-start.90
  487.6 7.1 collective-permute-start.91
  517.7 7.0 collective-permute-start.98
  519.0 7.1 collective-permute-start.99
  533.7 7.1 collective-permute-start.102
  535.0 7.1 collective-permute-start.103
  549.8 7.3 collective-permute-start.110
  551.1 7.1 collective-permute-start.111
  576.6 7.0 collective-permute-start.114
  577.9 7.1 collective-permute-start.115
  592.2 7.0 collective-permute-start.118
  593.5 7.1 collective-permute-start.119
  609.1 7.1 collective-permute-start.123
  623.4 7.1 collective-permute-start.126
  624.7 7.1 collective-permute-start.127
  760.4 7.1 collective-permute-start.143
  776.0 7.1 collective-permute-start.146
  793.2 7.1 collective-permute-start.151
  809.1 7.1 collective-permute-start.155
  823.8 7.0 collective-permute-start.158
  825.1 7.1 collective-permute-start.159
  839.7 7.0 collective-permute-start.162
  841.0 7.1 collective-permute-start.163
  (203 other events, 3407.4 us)
where the time goes:
time: 866 us; the launch traced here: 850 us
  starting transfers between devices  513 us (59%)
  blocking collectives  150 us (17%)
  waiting for transfers between devices  81.5 us (9%)
  local copies, waits for them, and re-layouts  59.3 us (7%)
  other arithmetic  39.7 us (5%)
    ppermute x82, starting transfers between devices, extended(): lax.ppermute(tail, axis, [(i, (i + 1) % count) for i in range(ends)])  407 us
    all_gather x2, blocking collectives, body(): whole = lax.all_gather(bundle[None], ('gx', 'gy'), axis=0, tiled=True)  150 us
    ppermute x82, starting transfers between devices, extended(): lax.ppermute(head, axis, [((i + 1) % count, i) for i in range(ends)])  106 us
    ppermute x82, waiting for transfers between devices, extended(): lax.ppermute(tail, axis, [(i, (i + 1) % count) for i in range(ends)])  76.9 us
    another operation x13, local copies, waits for them, and re-layouts, motion_tensor(): jnp.stack([scale * slopes[0] * slopes[0], scale * slopes[0] * slopes[1],...  20.6 us
  transfers between devices with their start and end apart: 164, of which 74 were waited for; matrix products, arithmetic and copies ran while one was open for 1% of the time, Pallas kernels for 0%

commit v1 on v0

v1 whole, which is shorter than its diff:
```python
import functools

import jax
import jax.numpy as jnp
from jax import lax
from jax.experimental import pallas as pl
from jax.experimental.pallas import tpu as pltpu
from jax.sharding import PartitionSpec as P

SWEEPS = 4
COARSE_SWEEPS = 12
CYCLES = 2
damping = 0.6
smooth_weight = 2.0
edge_scale = 0.25
floor_grad = 0.5
TINY = 1e-30

MESH = pl.DeviceIdType.MESH
SIDES = ((-1, 0), (1, 0), (0, -1), (0, 1))
AROUND = tuple((i, j) for i in (-1, 0, 1) for j in (-1, 0, 1) if (i, j) != (0, 0))
FINE_ROUNDS = 2 + 2 * SWEEPS
BLOCK_ROUNDS = 4


def sym(m, v):
    return [
        m[0] * v[0] + m[1] * v[1] + m[2] * v[2],
        m[1] * v[0] + m[3] * v[1] + m[4] * v[2],
        m[2] * v[0] + m[4] * v[1] + m[5] * v[2],
    ]


def damped_inverse(t, total):
    a, b, c, d, e, f = t[0] + total, t[1], t[2], t[3] + total, t[4], t[5] + total
    cof = [
        d * f - e * e,
        c * e - b * f,
        b * e - c * d,
        a * f - c * c,
        b * c - a * e,
        a * d - b * b,
    ]
    det = a * cof[0] + b * cof[1] + c * cof[2]
    factor = damping / jnp.where(total > 0.0, det, 1.0)
    return [factor * value for value in cof]


def kernel(
    GX, GY, NR, first_ref, second_ref, start_ref, flow_ref,
    mean_ref, weight_ref, tensor_ref, source_ref, face_ref, inv_ref,
    mid_t, mid_w, mid_face, mid_inv, mid_src, err,
    coarse_inv, coarse_src, corr,
    xh, yh, ys, bs, br, gs, gb,
    f_send, f_recv, b_send, b_recv, g_send, g_recv,
):
    gx = lax.axis_index("gx")
    gy = lax.axis_index("gy")
    me = gx * GY + gy
    n = GX * GY
    GT = GY // 8
    NM = NR // 2
    WR = 3 * NM
    shape = (8, 128)
    lane = lax.broadcasted_iota(jnp.int32, shape, 1)
    sub = lax.broadcasted_iota(jnp.int32, shape, 0)
    zero = jnp.zeros(shape, jnp.float32)

    def lroll(v, k):
        return pltpu.roll(v, k % 128, 1)

    def sroll(v, k):
        return pltpu.roll(v, k % 8, 0)

    def lane_bit(k):
        return (lane & k) == 0

    def sub_bit(k):
        return (sub & k) == 0

    def lane_pair(v, k):
        return v + jnp.where(lane_bit(k), lroll(v, -k), lroll(v, k))

    def sub_pair(v, k):
        return v + jnp.where(sub_bit(k), sroll(v, -k), sroll(v, k))

    def zup(v, k):
        return jnp.where(lane < 128 - k, lroll(v, -k), 0.0)

    def zdn(v, k):
        return jnp.where(lane >= k, lroll(v, k), 0.0)

    def y_shifts(tiles, k):
        count = len(tiles)
        ups = [sroll(v, -k) for v in tiles] + [zero]
        downs = [zero] + [sroll(v, k) for v in tiles]
        return (
            [jnp.where(sub < 8 - k, ups[j], ups[j + 1]) for j in range(count)],
            [jnp.where(sub >= k, downs[j + 1], downs[j]) for j in range(count)],
        )

    def here(dx, dy):
        conds = []
        if dx:
            conds.append((gx + dx >= 0) & (gx + dx < GX))
        if dy:
            conds.append((gy + dy >= 0) & (gy + dy < GY))
        return functools.reduce(lambda p, q: p & q, conds)

    for ref in (xh, yh, br, corr):
        flat = 1
        for extent in ref.shape[:-2]:
            flat *= extent
        ref[...] = jnp.zeros(ref.shape, jnp.float32)

    barrier = pltpu.get_barrier_semaphore()

    def greet(d, carry):
        other = lax.rem(me + d, n)
        pl.semaphore_signal(
            barrier, inc=1, device_id=(other // GY, lax.rem(other, GY)), device_id_type=MESH
        )
        return carry

    lax.fori_loop(1, n, greet, 0)
    pl.semaphore_wait(barrier, n - 1)

    def side_copy(ref, count, slot, k):
        dx, dy = SIDES[k]
        back = k ^ 1
        if dx:
            src = ref.at[pl.ds(0, count), 0 if dx < 0 else NR - 1]
            dst = xh.at[slot, back, pl.ds(0, count)]
        else:
            src = ys.at[slot, k - 2, pl.ds(0, count)]
            dst = yh.at[slot, back - 2, pl.ds(0, count)]
        return pltpu.make_async_remote_copy(
            src_ref=src, dst_ref=dst,
            send_sem=f_send.at[slot, k], recv_sem=f_recv.at[slot, back],
            device_id=(gx + dx, gy + dy), device_id_type=MESH,
        )

    def side_arrival(ref, count, slot, k):
        dx, dy = SIDES[k]
        if dx:
            dst = xh.at[slot, k, pl.ds(0, count)]
        else:
            dst = yh.at[slot, k - 2, pl.ds(0, count)]
        return pltpu.make_async_remote_copy(
            src_ref=dst, dst_ref=dst,
            send_sem=f_send.at[slot, k], recv_sem=f_recv.at[slot, k],
            device_id=(gx + dx, gy + dy), device_id_type=MESH,
        )

    def fine_start(ref, count, slot):
        for c in range(count):
            ys[slot, 0, c] = ref[c, :, 0, :]
            ys[slot, 1, c] = ref[c, :, 7, :]
        for k in (2, 3, 0, 1):
            @pl.when(here(*SIDES[k]))
            def _(k=k):
                side_copy(ref, count, slot, k).start()

    def fine_wait(ref, count, slot):
        for k in (0, 1, 2, 3):
            @pl.when(here(*SIDES[k]))
            def _(k=k):
                side_arrival(ref, count, slot, k).wait_recv()
                side_copy(ref, count, slot, k).wait_send()

    def block_copy(count, slot, k):
        dx, dy = AROUND[k]
        return pltpu.make_async_remote_copy(
            src_ref=bs.at[slot, pl.ds(0, count)],
            dst_ref=br.at[slot, 7 - k, pl.ds(0, count)],
            send_sem=b_send.at[slot, k], recv_sem=b_recv.at[slot, 7 - k],
            device_id=(gx + dx, gy + dy), device_id_type=MESH,
        )

    def block_arrival(count, slot, k):
        dx, dy = AROUND[k]
        dst = br.at[slot, k, pl.ds(0, count)]
        return pltpu.make_async_remote_copy(
            src_ref=dst, dst_ref=dst,
            send_sem=b_send.at[slot, k], recv_sem=b_recv.at[slot, k],
            device_id=(gx + dx, gy + dy), device_id_type=MESH,
        )

    def pack(rows):
        lower = jnp.where(lane_bit(1), rows[0], rows[1])
        upper = jnp.where(lane_bit(1), rows[2], rows[3])
        return jnp.where(sub_bit(1), lower, upper)

    def unpack(v):
        even = jnp.where(lane_bit(1), v, lroll(v, 1))
        odd = jnp.where(lane_bit(1), lroll(v, -1), v)

        def split(w):
            return (
                jnp.where(sub_bit(1), w, sroll(w, 1)),
                jnp.where(sub_bit(1), sroll(w, -1), w),
            )

        e, o = split(even), split(odd)
        return [e[0], o[0], e[1], o[1]]

    def block_start(fields, slot):
        for i, rows in enumerate(fields):
            bs[slot, i] = pack(rows)
        for k in range(8):
            @pl.when(here(*AROUND[k]))
            def _(k=k):
                block_copy(len(fields), slot, k).start()

    def block_wait(count, slot):
        for k in range(8):
            @pl.when(here(*AROUND[k]))
            def _(k=k):
                block_arrival(count, slot, k).wait_recv()
                block_copy(count, slot, k).wait_send()

    def block_spread(places, slot):
        for k, (dx, dy) in enumerate(AROUND):
            for i, place in enumerate(places):
                for r, v in enumerate(unpack(br[slot, k, i])):
                    place[NM * (dx + 1) + r, dy + 1] = v

    def keep_own(place, rows):
        for r, v in enumerate(rows):
            place[NM + r, 1] = v

    def gather_copy(slot, other):
        return pltpu.make_async_remote_copy(
            src_ref=gs.at[slot], dst_ref=gb.at[slot, me],
            send_sem=g_send.at[slot], recv_sem=g_recv.at[slot],
            device_id=(other // GY, lax.rem(other, GY)), device_id_type=MESH,
        )

    def gather_start(values, slot):
        row = zero
        for i, v in enumerate(values):
            row = jnp.where((lane & 7) == i, v, row)
        gs[slot] = row[0:1]
        gb[slot, me] = row[0:1]

        def send(d, carry):
            gather_copy(slot, lax.rem(me + d, n)).start()
            return carry

        lax.fori_loop(1, n, send, 0)

    def gather_wait(slot):
        whole = gb.at[slot, pl.ds(0, n - 1)]
        copy = pltpu.make_async_remote_copy(
            src_ref=whole, dst_ref=whole,
            send_sem=g_send.at[slot], recv_sem=g_recv.at[slot],
            device_id=(gx, gy), device_id_type=MESH,
        )
        copy.wait_recv()
        copy.wait_send()

    def gathered(slot, count, g, t):
        packed = gb[slot, pl.ds(g * GY + t * 8, 8), 0, :]
        result = []
        for i in range(count):
            v = jnp.where((lane & 7) == i, packed, 0.0)
            for k in (1, 2, 4):
                v = lane_pair(v, k)
            result.append(v)
        return result

    def restrict_fine(rows):
        result = []
        for m in range(NM):
            v = rows[2 * m] + rows[2 * m + 1]
            result.append(sub_pair(lane_pair(v, 1), 1) * 0.125)
        return result

    def restrict_mid(rows):
        v = functools.reduce(lambda p, q: p + q, rows)
        for k in (2, 4):
            v = lane_pair(v, k)
            v = sub_pair(v, k)
        return v * (1.0 / 64.0)

    def fine_rows(ref, c, slot):
        return [xh[slot, 0, c]] + [ref[c, x] for x in range(NR)] + [xh[slot, 1, c]]

    def fine_y(rows, c, slot, x):
        v = rows[x + 1]
        up = jnp.where(sub < 7, sroll(v, -1), yh[slot, 1, c, x:x + 1, :])
        down = jnp.where(sub >= 1, sroll(v, 1), yh[slot, 0, c, x:x + 1, :])
        return up, down

    for x in range(NR):
        mean_ref[0, x] = 0.5 * (first_ref[x] + second_ref[x])
        for c in range(3):
            flow_ref[c, x] = start_ref[c, x]
    fine_start(mean_ref, 1, 0)
    fine_wait(mean_ref, 1, 0)
    rows = fine_rows(mean_ref, 0, 0)
    for x in range(NR):
        up, down = fine_y(rows, 0, 0, x)
        s0 = 0.5 * (rows[x + 2] - rows[x])
        s1 = 0.5 * (up - down)
        s2 = 0.5 * (zup(rows[x + 1], 1) - zdn(rows[x + 1], 1))
        change = second_ref[x] - first_ref[x]
        scale = 1.0 / (s0 * s0 + s1 * s1 + s2 * s2 + floor_grad)
        a0, a1, a2 = scale * s0, scale * s1, scale * s2
        for i, v in enumerate((a0 * s0, a0 * s1, a0 * s2, a1 * s1, a1 * s2, a2 * s2)):
            tensor_ref[i, x] = v
        for i, v in enumerate((a0, a1, a2)):
            source_ref[i, x] = -v * change
    mids, coarses = [], []
    for i in range(6):
        own = restrict_fine([tensor_ref[i, x] for x in range(NR)])
        keep_own(mid_t.at[i], own)
        mids.append(own)
        coarses.append(restrict_mid(own))
    block_start(mids, 0)
    gather_start(coarses, 0)
    block_wait(6, 0)
    block_spread([mid_t.at[i] for i in range(6)], 0)
    gather_wait(0)
    cface = smooth_weight / 64.0
    for g in range(GX):
        for t in range(GT):
            tensor = gathered(0, 6, g, t)
            count = jnp.where(lane < 120, 1.0, 0.0) + jnp.where(lane >= 8, 1.0, 0.0)
            count = count + jnp.where(sub + t * 8 < GY - 1, 1.0, 0.0)
            count = count + jnp.where(sub + t * 8 >= 1, 1.0, 0.0)
            count = count + float((g > 0) + (g < GX - 1))
            for i, v in enumerate(damped_inverse(tensor, cface * count)):
                coarse_inv[i, g, t] = v

    def fine_inflow(x, all_rows, slot):
        flows = []
        face = [face_ref[i, x] for i in range(6)]
        for c in range(3):
            rows = all_rows[c]
            up, down = fine_y(rows, c, slot, x)
            v = source_ref[c, x] + face[0] * rows[x + 2] + face[1] * rows[x]
            v = v + face[2] * up + face[3] * down
            v = v + face[4] * lroll(rows[x + 1], -1) + face[5] * lroll(rows[x + 1], 1)
            flows.append(v)
        return flows, face

    def fine_relax(slot):
        all_rows = [fine_rows(flow_ref, c, slot) for c in range(3)]
        for x in range(NR):
            flows, _ = fine_inflow(x, all_rows, slot)
            out = sym([inv_ref[i, x] for i in range(6)], flows)
            for c in range(3):
                flow_ref[c, x] = (1.0 - damping) * all_rows[c][x + 1] + out[c]

    def mid_inflow(r, p, tiles, wanted):
        flows = [[None] * 3 for _ in range(3)]
        for c in range(3):
            now = [err[p, c, r, j] for j in range(3)]
            tiles[c] = now
            ups, downs = y_shifts(now, 2)
            for j in wanted:
                v = mid_src[c, r, j] + mid_face[0, r, j] * err[p, c, r + 1, j]
                v = v + mid_face[1, r, j] * err[p, c, r - 1, j]
                v = v + mid_face[2, r, j] * ups[j] + mid_face[3, r, j] * downs[j]
                v = v + mid_face[4, r, j] * lroll(now[j], -2)
                flows[c][j] = v + mid_face[5, r, j] * lroll(now[j], 2)
        return flows

    def mid_relax(p, low):
        def turn(r, carry):
            tiles = [None] * 3
            flows = mid_inflow(r, p, tiles, (0, 1, 2))
            for j in range(3):
                out = sym([mid_inv[i, r, j] for i in range(6)], [flows[c][j] for c in range(3)])
                for c in range(3):
                    err[1 - p, c, r, j] = (1.0 - damping) * tiles[c][j] + out[c]
            return carry

        lax.fori_loop(low, WR - low, turn, 0)

    def mid_prepare():
        scale = 2.0 * smooth_weight / 4.0

        def turn(r, carry):
            now = [mid_w[r, j] for j in range(3)]
            has_up = jnp.where(r < WR - 1, 1.0, 0.0)
            has_down = jnp.where(r > 0, 1.0, 0.0)
            above = jnp.minimum(r + 1, WR - 1)
            below = jnp.maximum(r - 1, 0)
            ups, downs = y_shifts(now, 2)
            for j in range(3):
                v = now[j]
                beside = [
                    mid_w[above, j] * has_up, mid_w[below, j] * has_down,
                    ups[j], downs[j], zup(v, 2), zdn(v, 2),
                ]
                face = [scale * v * o / jnp.maximum(v + o, TINY) for o in beside]
                total = functools.reduce(lambda p, q: p + q, face)
                for i in range(6):
                    mid_face[i, r, j] = face[i]
                tensor = [mid_t[i, r, j] for i in range(6)]
                for i, w in enumerate(damped_inverse(tensor, total)):
                    mid_inv[i, r, j] = w
            return carry

        lax.fori_loop(0, WR, turn, 0)

    def cycle(cyc, carry):
        base = 1 + cyc * FINE_ROUNDS
        bbase = 1 + cyc * BLOCK_ROUNDS
        fine_start(flow_ref, 3, base)
        fine_wait(flow_ref, 3, base)
        q = [zero] * NR
        for c in range(3):
            rows = fine_rows(flow_ref, c, base)
            for x in range(NR):
                up, down = fine_y(rows, c, base, x)
                s0 = 0.5 * (rows[x + 2] - rows[x])
                s1 = 0.5 * (up - down)
                s2 = 0.5 * (zup(rows[x + 1], 1) - zdn(rows[x + 1], 1))
                q[x] = q[x] + s0 * s0 + s1 * s1 + s2 * s2
        weights = [lax.rsqrt(1.0 + v * (1.0 / edge_scale)) for v in q]
        for x in range(NR):
            weight_ref[0, x] = weights[x]
        fine_start(weight_ref, 1, base + 1)
        own_w = restrict_fine(weights)
        keep_own(mid_w, own_w)
        block_start([own_w], bbase)
        fine_wait(weight_ref, 1, base + 1)
        rows = fine_rows(weight_ref, 0, base + 1)
        for x in range(NR):
            v = rows[x + 1]
            up, down = fine_y(rows, 0, base + 1, x)
            beside = [rows[x + 2], rows[x], up, down, zup(v, 1), zdn(v, 1)]
            face = [2.0 * smooth_weight * v * o / (v + o) for o in beside]
            total = functools.reduce(lambda p, q: p + q, face)
            for i in range(6):
                face_ref[i, x] = face[i]
            tensor = [tensor_ref[i, x] for i in range(6)]
            for i, w in enumerate(damped_inverse(tensor, total)):
                inv_ref[i, x] = w
        fine_relax(base)
        for sweep in range(1, SWEEPS):
            slot = base + 1 + sweep
            fine_start(flow_ref, 3, slot)
            if sweep == 1:
                block_wait(1, bbase)
                block_spread([mid_w], bbase)
                mid_prepare()
            fine_wait(flow_ref, 3, slot)
            fine_relax(slot)
        slot = base + 1 + SWEEPS
        fine_start(flow_ref, 3, slot)
        fine_wait(flow_ref, 3, slot)
        all_rows = [fine_rows(flow_ref, c, slot) for c in range(3)]
        rest = [[], [], []]
        for x in range(NR):
            flows, face = fine_inflow(x, all_rows, slot)
            total = functools.reduce(lambda p, q: p + q, face)
            now = [all_rows[c][x + 1] for c in range(3)]
            out = sym([tensor_ref[i, x] for i in range(6)], now)
            for c in range(3):
                rest[c].append(flows[c] - out[c] - total * now[c])
        srcs = [restrict_fine(rest[c]) for c in range(3)]
        errs = [[], [], []]
        for r in range(NM):
            out = sym([mid_inv[i, NM + r, 1] for i in range(6)], [srcs[c][r] for c in range(3)])
            for c in range(3):
                errs[c].append(out[c])
        block_start(srcs + errs, bbase + 1)
        for c in range(3):
            keep_own(mid_src.at[c], srcs[c])
            keep_own(err.at[0, c], errs[c])
        block_wait(6, bbase + 1)
        block_spread([mid_src.at[c] for c in range(3)] + [err.at[0, c] for c in range(3)], bbase + 1)
        p = 0
        for sweep in range(1, SWEEPS):
            mid_relax(p, sweep)
            p = 1 - p
        mrest = [[], [], []]
        olds = [[], [], []]
        for r in range(NM, 2 * NM):
            tiles = [None] * 3
            flows = mid_inflow(r, p, tiles, (1,))
            total = functools.reduce(lambda a, b: a + b, [mid_face[i, r, 1] for i in range(6)])
            now = [tiles[c][1] for c in range(3)]
            out = sym([mid_t[i, r, 1] for i in range(6)], now)
            for c in range(3):
                mrest[c].append(flows[c][1] - out[c] - total * now[c])
                olds[c].append(now[c])
        gather_start([restrict_mid(mrest[c]) for c in range(3)], 1 + cyc)
        block_start(olds, bbase + 2)
        block_wait(3, bbase + 2)
        block_spread([err.at[p, c] for c in range(3)], bbase + 2)
        gather_wait(1 + cyc)

        current = []
        for g in range(GX):
            for t in range(GT):
                src = gathered(1 + cyc, 3, g, t)
                out = sym([coarse_inv[i, g, t] for i in range(6)], src)
                for c in range(3):
                    coarse_src[c, g, t] = src[c]
                current.append(out)

        def coarse_turn(index, now):
            result = []
            for g in range(GX):
                shifted = [
                    y_shifts([now[g * GT + t][c] for t in range(GT)], 1) for c in range(3)
                ]
                for t in range(GT):
                    flows = []
                    for c in range(3):
                        v = now[g * GT + t][c]
                        s = shifted[c][0][t] + shifted[c][1][t]
                        s = s + (zup(v, 8) + zdn(v, 8))
                        if g > 0:
                            s = s + now[(g - 1) * GT + t][c]
                        if g < GX - 1:
                            s = s + now[(g + 1) * GT + t][c]
                        flows.append(coarse_src[c, g, t] + cface * s)
                    out = sym([coarse_inv[i, g, t] for i in range(6)], flows)
                    result.append(
                        [(1.0 - damping) * now[g * GT + t][c] + out[c] for c in range(3)]
                    )
            return result

        current = lax.fori_loop(0, COARSE_SWEEPS - 1, coarse_turn, current)
        ratio = NM
        step = (lane // 2) & 3
        lane_far = jnp.where((step == 0) | (step == 3), 0.375, 0.125)
        sub_far = jnp.where(((sub // 2) == 0) | ((sub // 2) == 3), 0.375, 0.125)
        for g in range(GX):
            for t in range(GT):
                for c in range(3):
                    v = current[g * GT + t][c]
                    other = jnp.where(step < 2, zdn(v, 8), zup(v, 8))
                    corr[c, 2 + g, 8 + 8 * t:16 + 8 * t, :] = (1.0 - lane_far) * v + lane_far * other
        for c in range(3):
            columns = []
            for i in range(5):
                cells = [
                    jnp.broadcast_to(corr[c, gx + i, pl.ds(gy + 6 + j, 1), :], shape)
                    for j in range(5)
                ]
                columns.append([
                    (1.0 - sub_far) * cells[j] + sub_far * jnp.where(sub < 4, cells[j - 1], cells[j + 1])
                    for j in (1, 2, 3)
                ])
            for r in range(WR):
                b, d = r // ratio + 1, r % ratio
                shift = (d + 0.5) / ratio - 0.5
                o = b - 1 if shift < 0 else b + 1
                for j in range(3):
                    lifted = (1.0 - abs(shift)) * columns[b][j] + abs(shift) * columns[o][j]
                    err[p, c, r, j] = err[p, c, r, j] + lifted
        for sweep in range(1, SWEEPS + 1):
            mid_relax(p, sweep)
            p = 1 - p
        block_start(
            [[err[p, c, NM + r, 1] for r in range(NM)] for c in range(3)], bbase + 3
        )
        block_wait(3, bbase + 3)
        block_spread([err.at[p, c] for c in range(3)], bbase + 3)
        for c in range(3):
            raised = []
            for r in range(NM - 1, 2 * NM + 1):
                tiles = [err[p, c, r, j] for j in range(3)]
                ups, downs = y_shifts(tiles, 2)
                v = 0.75 * tiles[1] + 0.25 * jnp.where(sub_bit(1), downs[1], ups[1])
                v = 0.75 * v + 0.25 * jnp.where(lane_bit(1), zdn(v, 2), zup(v, 2))
                raised.append(v)
            for x in range(NR):
                m = x // 2 + 1
                o = m - 1 if x % 2 == 0 else m + 1
                flow_ref[c, x] = flow_ref[c, x] + 0.75 * raised[m] + 0.25 * raised[o]
        for sweep in range(SWEEPS):
            slot = base + 2 + SWEEPS + sweep
            fine_start(flow_ref, 3, slot)
            fine_wait(flow_ref, 3, slot)
            fine_relax(slot)
        return carry

    lax.fori_loop(0, CYCLES, cycle, 0)


def solution(mesh):
    GX, GY = mesh.shape["gx"], mesh.shape["gy"]

    def body(first_image, second_image, start_flow):
        NR, cols, depth = first_image.shape
        assert NR == 8 and cols == 8 and depth == 128 and GY % 8 == 0
        rounds = 1 + CYCLES * FINE_ROUNDS
        blocks = 1 + CYCLES * BLOCK_ROUNDS
        WR = 3 * NR // 2
        f32 = jnp.float32
        tile = (8, 128)
        vmem = lambda *front: pltpu.VMEM(front + tile, f32)
        return pl.pallas_call(
            functools.partial(kernel, GX, GY, NR),
            out_shape=jax.ShapeDtypeStruct(start_flow.shape, f32),
            in_specs=[pl.BlockSpec(memory_space=pltpu.VMEM)] * 3,
            out_specs=pl.BlockSpec(memory_space=pltpu.VMEM),
            scratch_shapes=[
                vmem(1, NR), vmem(1, NR), vmem(6, NR), vmem(3, NR), vmem(6, NR), vmem(6, NR),
                vmem(6, WR, 3), vmem(WR, 3), vmem(6, WR, 3), vmem(6, WR, 3), vmem(3, WR, 3),
                vmem(2, 3, WR, 3),
                vmem(6, GX, GY // 8), vmem(3, GX, GY // 8),
                pltpu.VMEM((3, GX + 4, GY + 16, 128), f32),
                vmem(rounds, 2, 3), vmem(rounds, 2, 3), vmem(rounds, 2, 3),
                vmem(blocks, 6), vmem(blocks, 8, 6),
                pltpu.VMEM((1 + CYCLES, 1, 128), f32),
                pltpu.VMEM((1 + CYCLES, GX * GY, 1, 128), f32),
                pltpu.SemaphoreType.DMA((rounds, 4)), pltpu.SemaphoreType.DMA((rounds, 4)),
                pltpu.SemaphoreType.DMA((blocks, 8)), pltpu.SemaphoreType.DMA((blocks, 8)),
                pltpu.SemaphoreType.DMA((1 + CYCLES,)), pltpu.SemaphoreType.DMA((1 + CYCLES,)),
            ],
            compiler_params=pltpu.CompilerParams(
                collective_id=0, has_side_effects=True, vmem_limit_bytes=48 * 1024 * 1024
            ),
            name="flow_cycles",
        )(first_image, second_image, start_flow)

    return jax.shard_map(
        body,
        mesh=mesh,
        in_specs=(P("gx", "gy", None), P("gx", "gy", None), P(None, "gx", "gy", None)),
        out_specs=P(None, "gx", "gy", None),
        check_vma=False,
    )
```

time: 866 us -> 124 us (0.14); the launches traced: 850 us -> 124 us
  starting transfers between devices: 513 us -> 0 us
  blocking collectives: 150 us -> 0 us
  Pallas kernels: 0 us -> 120 us
  waiting for transfers between devices: 81.5 us -> 0 us
  local copies, waits for them, and re-layouts: 59.3 us -> 3.05 us
  other arithmetic: 39.7 us -> 0 us
    ppermute x164 -> x0, starting transfers between devices: 513 us -> none  [the longest x82 407 us: extended(): lax.ppermute(tail, axis, [(i, (i + 1) % count) for i in range(ends)])]
    all_gather x2 -> x0, blocking collectives: 150 us -> none  [body(): whole = lax.all_gather(bundle[None], ('gx', 'gy'), axis=0, tiled=True)]
    pallas_call x0 -> x1, Pallas kernels: none -> 120 us  [body(): pl.pallas_call(functools.partial(kernel, GX, GY, NR), out_shape=jax.Shape...]
    ppermute x164 -> x0, waiting for transfers between devices: 81.5 us -> none  [the longest x82 76.9 us: extended(): lax.ppermute(tail, axis, [(i, (i + 1) % count) for i in range(ends)])]
    another operation x22 -> x0, local copies, waits for them, and re-layouts: 22.9 us -> none  [the longest x13 20.6 us: motion_tensor(): jnp.stack([scale * slopes[0] * slopes[0], scale * slopes[0] * slopes[1],...]
    reshape x11 -> x0, local copies, waits for them, and re-layouts: 16.9 us -> none  [the longest x2 15.2 us: restrict(): field.reshape(front + (across // ratio, ratio, along // ratio, ratio, dep...]
    concatenate x80 -> x0, other arithmetic: 11 us -> none  [the longest x78 11 us: extended(): jnp.concatenate([lax.ppermute(tail, axis, [(i, (i + 1) % count) for i in...]
    add x171 -> x0, other arithmetic: 11 us -> none  [the longest x52 6.3 us: relaxed(): source + inflow(padded_field, level)]
  transfers between devices with their start and end apart: 164 -> 0, of which waited for: 74 -> 0; matrix products, arithmetic and copies ran while one was open for 1% -> 0% of each run, Pallas kernels for 0% -> 0%
where the time goes in v1:
time: 124 us
  Pallas kernels  120 us (97%)
  local copies, waits for them, and re-layouts  3.05 us (2%)
    pallas_call x1, Pallas kernels, body(): pl.pallas_call(functools.partial(kernel, GX, GY, NR), out_shape=jax.Shape...  120 us
    unnamed x7, local copies, waits for them, and re-layouts  3.05 us

profile of v1, /device:TPU:0, one launch (start us, length us, event | category | flops | bytes accessed | tf_op | source)
XLA Modules:
  0.0 123.5 jit_solution(7704422861710212189)
XLA Ops:
  0.0 0.0 copy-start
  0.0 0.9 copy-done
  0.9 0.0 copy-start.1
  0.9 0.8 copy-done.1
  1.7 0.0 copy-start.2
  1.7 0.8 copy-done.2
  2.4 120.5 %flow_cycles.1 = f32[3,8,8,128]{3,2,1,0:T(8,128)S(1)} custom-call(f32[8,8,128]{2,1,0:T(8,128)S(1)} %copy-done.1, f32[8,8,128]{2,1,0:T(8,128)S(1)} %copy-done.2, f32[3,8,8,128]{3,2,1,0:T(8,128)S(1)} %copy-done), custom_call_target="tpu_custom_call" | custom-call | tf_op jit(solution)/shard_map/flow_cycles/pallas_call | solution.py:601
  122.9 0.6 copy.5
Async XLA Ops:
  0.0 0.9 copy-start
  0.9 0.8 copy-start.1
  1.7 0.8 copy-start.2

commit v2 on v1

--- a/solution.py
+++ b/solution.py
@@ -51,7 +51,7 @@
     mean_ref, weight_ref, tensor_ref, source_ref, face_ref, inv_ref,
     mid_t, mid_w, mid_face, mid_inv, mid_src, err,
     coarse_inv, coarse_src, corr,
-    xh, yh, ys, bs, br, gs, gb,
+    xh, yh, xs, ys, bs, br, gs, gb,
     f_send, f_recv, b_send, b_recv, g_send, g_recv,
 ):
     gx = lax.axis_index("gx")
@@ -129,7 +129,7 @@
         dx, dy = SIDES[k]
         back = k ^ 1
         if dx:
-            src = ref.at[pl.ds(0, count), 0 if dx < 0 else NR - 1]
+            src = xs.at[slot, k, pl.ds(0, count)]
             dst = xh.at[slot, back, pl.ds(0, count)]
         else:
             src = ys.at[slot, k - 2, pl.ds(0, count)]
@@ -156,6 +156,8 @@
         for c in range(count):
             ys[slot, 0, c] = ref[c, :, 0, :]
             ys[slot, 1, c] = ref[c, :, 7, :]
+            xs[slot, 0, c] = ref[c, 0]
+            xs[slot, 1, c] = ref[c, NR - 1]
         for k in (2, 3, 0, 1):
             @pl.when(here(*SIDES[k]))
             def _(k=k):
@@ -297,6 +299,7 @@
         for c in range(3):
             flow_ref[c, x] = start_ref[c, x]
     fine_start(mean_ref, 1, 0)
+    fine_start(flow_ref, 3, 1)
     fine_wait(mean_ref, 1, 0)
     rows = fine_rows(mean_ref, 0, 0)
     for x in range(NR):
@@ -319,11 +322,18 @@
         coarses.append(restrict_mid(own))
     block_start(mids, 0)
     gather_start(coarses, 0)
-    block_wait(6, 0)
-    block_spread([mid_t.at[i] for i in range(6)], 0)
-    gather_wait(0)
     cface = smooth_weight / 64.0
-    for g in range(GX):
+
+    def mid_arrives():
+        block_wait(6, 0)
+        block_spread([mid_t.at[i] for i in range(6)], 0)
+
+    def coarse_arrives():
+        gather_wait(0)
+        for g in range(GX):
+            coarse_row(g)
+
+    def coarse_row(g):
         for t in range(GT):
             tensor = gathered(0, 6, g, t)
             count = jnp.where(lane < 120, 1.0, 0.0) + jnp.where(lane >= 8, 1.0, 0.0)
@@ -345,13 +355,36 @@
             flows.append(v)
         return flows, face
 
-    def fine_relax(slot):
-        all_rows = [fine_rows(flow_ref, c, slot) for c in range(3)]
+    def fine_inside():
+        rows = [[flow_ref[c, x] for x in range(NR)] for c in range(3)]
         for x in range(NR):
-            flows, _ = fine_inflow(x, all_rows, slot)
+            flows = []
+            for c in range(3):
+                now = rows[c][x]
+                v = source_ref[c, x] + face_ref[4, x] * lroll(now, -1)
+                v = v + face_ref[5, x] * lroll(now, 1)
+                v = v + face_ref[2, x] * jnp.where(sub < 7, sroll(now, -1), 0.0)
+                v = v + face_ref[3, x] * jnp.where(sub >= 1, sroll(now, 1), 0.0)
+                if x < NR - 1:
+                    v = v + face_ref[0, x] * rows[c][x + 1]
+                if x > 0:
+                    v = v + face_ref[1, x] * rows[c][x - 1]
+                flows.append(v)
             out = sym([inv_ref[i, x] for i in range(6)], flows)
             for c in range(3):
-                flow_ref[c, x] = (1.0 - damping) * all_rows[c][x + 1] + out[c]
+                flow_ref[c, x] = (1.0 - damping) * rows[c][x] + out[c]
+
+    def fine_edges(slot):
+        for side, x, face in ((0, 0, 1), (1, NR - 1, 0)):
+            outer = [face_ref[face, x] * xh[slot, side, c] for c in range(3)]
+            out = sym([inv_ref[i, x] for i in range(6)], outer)
+            for c in range(3):
+                flow_ref[c, x] = flow_ref[c, x] + out[c]
+        for side, y, face in ((0, 0, 3), (1, 7, 2)):
+            outer = [face_ref[face, :, y, :] * yh[slot, side, c] for c in range(3)]
+            out = sym([inv_ref[i, :, y, :] for i in range(6)], outer)
+            for c in range(3):
+                flow_ref[c, :, y, :] = flow_ref[c, :, y, :] + out[c]
 
     def mid_inflow(r, p, tiles, wanted):
         flows = [[None] * 3 for _ in range(3)]
@@ -369,15 +402,21 @@
 
     def mid_relax(p, low):
         def turn(r, carry):
-            tiles = [None] * 3
-            flows = mid_inflow(r, p, tiles, (0, 1, 2))
-            for j in range(3):
-                out = sym([mid_inv[i, r, j] for i in range(6)], [flows[c][j] for c in range(3)])
-                for c in range(3):
-                    err[1 - p, c, r, j] = (1.0 - damping) * tiles[c][j] + out[c]
+            r = low + 2 * r
+            done = []
+            for u in range(2):
+                tiles = [None] * 3
+                flows = mid_inflow(r + u, p, tiles, (0, 1, 2))
+                for j in range(3):
+                    matrix = [mid_inv[i, r + u, j] for i in range(6)]
+                    out = sym(matrix, [flows[c][j] for c in range(3)])
+                    for c in range(3):
+                        done.append((c, u, j, (1.0 - damping) * tiles[c][j] + out[c]))
+            for c, u, j, v in done:
+                err[1 - p, c, r + u, j] = v
             return carry
 
-        lax.fori_loop(low, WR - low, turn, 0)
+        lax.fori_loop(0, (WR - 2 * low) // 2, turn, 0)
 
     def mid_prepare():
         scale = 2.0 * smooth_weight / 4.0
@@ -409,7 +448,11 @@
     def cycle(cyc, carry):
         base = 1 + cyc * FINE_ROUNDS
         bbase = 1 + cyc * BLOCK_ROUNDS
-        fine_start(flow_ref, 3, base)
+
+        @pl.when(cyc > 0)
+        def _():
+            fine_start(flow_ref, 3, base)
+
         fine_wait(flow_ref, 3, base)
         q = [zero] * NR
         for c in range(3):
@@ -440,16 +483,22 @@
             tensor = [tensor_ref[i, x] for i in range(6)]
             for i, w in enumerate(damped_inverse(tensor, total)):
                 inv_ref[i, x] = w
-        fine_relax(base)
+        fine_inside()
+        fine_edges(base)
         for sweep in range(1, SWEEPS):
             slot = base + 1 + sweep
             fine_start(flow_ref, 3, slot)
+            fine_inside()
             if sweep == 1:
                 block_wait(1, bbase)
                 block_spread([mid_w], bbase)
+                pl.when(cyc == 0)(mid_arrives)
+            if sweep == 2:
                 mid_prepare()
+            if sweep == 3:
+                pl.when(cyc == 0)(coarse_arrives)
             fine_wait(flow_ref, 3, slot)
-            fine_relax(slot)
+            fine_edges(slot)
         slot = base + 1 + SWEEPS
         fine_start(flow_ref, 3, slot)
         fine_wait(flow_ref, 3, slot)
@@ -579,8 +628,9 @@
         for sweep in range(SWEEPS):
             slot = base + 2 + SWEEPS + sweep
             fine_start(flow_ref, 3, slot)
+            fine_inside()
             fine_wait(flow_ref, 3, slot)
-            fine_relax(slot)
+            fine_edges(slot)
         return carry
 
     lax.fori_loop(0, CYCLES, cycle, 0)
@@ -609,7 +659,7 @@
                 vmem(2, 3, WR, 3),
                 vmem(6, GX, GY // 8), vmem(3, GX, GY // 8),
                 pltpu.VMEM((3, GX + 4, GY + 16, 128), f32),
-                vmem(rounds, 2, 3), vmem(rounds, 2, 3), vmem(rounds, 2, 3),
+                vmem(rounds, 2, 3), vmem(rounds, 2, 3), vmem(rounds, 2, 3), vmem(rounds, 2, 3),
                 vmem(blocks, 6), vmem(blocks, 8, 6),
                 pltpu.VMEM((1 + CYCLES, 1, 128), f32),
                 pltpu.VMEM((1 + CYCLES, GX * GY, 1, 128), f32),

time: 124 us -> 113 us (0.911)
  Pallas kernels: 120 us -> 109 us
    pallas_call x1, Pallas kernels: 120 us -> 109 us  [body(): pl.pallas_call(functools.partial(kernel, GX, GY, NR), out_shape=jax.Shape...]
where the time goes in v2:
time: 113 us; the launch traced here: 112 us
  Pallas kernels  109 us (96%)
  local copies, waits for them, and re-layouts  3.05 us (3%)
    pallas_call x1, Pallas kernels, body(): pl.pallas_call(functools.partial(kernel, GX, GY, NR), out_shape=jax.Shape...  109 us
    unnamed x7, local copies, waits for them, and re-layouts  3.05 us

profile of v2, /device:TPU:0, one launch (start us, length us, event | category | flops | bytes accessed | tf_op | source)
XLA Modules:
  0.0 112.4 jit_solution(850358424866890068)
XLA Ops:
  0.0 0.0 copy-start
  0.0 0.9 copy-done
  0.9 0.0 copy-start.1
  0.9 0.8 copy-done.1
  1.7 0.0 copy-start.2
  1.7 0.8 copy-done.2
  2.4 109.3 %flow_cycles.1 = f32[3,8,8,128]{3,2,1,0:T(8,128)S(1)} custom-call(f32[8,8,128]{2,1,0:T(8,128)S(1)} %copy-done.1, f32[8,8,128]{2,1,0:T(8,128)S(1)} %copy-done.2, f32[3,8,8,128]{3,2,1,0:T(8,128)S(1)} %copy-done), custom_call_target="tpu_custom_call" | custom-call | tf_op jit(solution)/shard_map/flow_cycles/pallas_call | solution.py:651
  111.8 0.6 copy.5
Async XLA Ops:
  0.0 0.9 copy-start
  0.9 0.8 copy-start.1
  1.7 0.8 copy-start.2

commit v3 on v2

--- a/solution.py
+++ b/solution.py
@@ -20,7 +20,7 @@
 SIDES = ((-1, 0), (1, 0), (0, -1), (0, 1))
 AROUND = tuple((i, j) for i in (-1, 0, 1) for j in (-1, 0, 1) if (i, j) != (0, 0))
 FINE_ROUNDS = 2 + 2 * SWEEPS
-BLOCK_ROUNDS = 4
+BLOCK_ROUNDS = 5
 
 
 def sym(m, v):
@@ -49,7 +49,7 @@
 def kernel(
     GX, GY, NR, first_ref, second_ref, start_ref, flow_ref,
     mean_ref, weight_ref, tensor_ref, source_ref, face_ref, inv_ref,
-    mid_t, mid_w, mid_face, mid_inv, mid_src, err,
+    mid_t, mid_w, mid_total, mid_face, mid_inv, mid_src, err,
     coarse_inv, coarse_src, corr,
     xh, yh, xs, ys, bs, br, gs, gb,
     f_send, f_recv, b_send, b_recv, g_send, g_recv,
@@ -438,9 +438,28 @@
                 total = functools.reduce(lambda p, q: p + q, face)
                 for i in range(6):
                     mid_face[i, r, j] = face[i]
+                mid_total[r, j] = total
+            return carry
+
+        lax.fori_loop(0, WR, turn, 0)
+
+    def mid_invert():
+        def turn(r, carry):
+            for j in range(3):
                 tensor = [mid_t[i, r, j] for i in range(6)]
-                for i, w in enumerate(damped_inverse(tensor, total)):
+                for i, w in enumerate(damped_inverse(tensor, mid_total[r, j])):
                     mid_inv[i, r, j] = w
+            return carry
+
+        lax.fori_loop(0, WR, turn, 0)
+
+    def mid_begin():
+        def turn(r, carry):
+            for j in range(3):
+                matrix = [mid_inv[i, r, j] for i in range(6)]
+                out = sym(matrix, [mid_src[c, r, j] for c in range(3)])
+                for c in range(3):
+                    err[0, c, r, j] = out[c]
             return carry
 
         lax.fori_loop(0, WR, turn, 0)
@@ -495,7 +514,11 @@
                 pl.when(cyc == 0)(mid_arrives)
             if sweep == 2:
                 mid_prepare()
+                block_start([[mid_total[NM + r, 1] for r in range(NM)]], bbase + 4)
             if sweep == 3:
+                block_wait(1, bbase + 4)
+                block_spread([mid_total], bbase + 4)
+                mid_invert()
                 pl.when(cyc == 0)(coarse_arrives)
             fine_wait(flow_ref, 3, slot)
             fine_edges(slot)
@@ -512,17 +535,12 @@
             for c in range(3):
                 rest[c].append(flows[c] - out[c] - total * now[c])
         srcs = [restrict_fine(rest[c]) for c in range(3)]
-        errs = [[], [], []]
-        for r in range(NM):
-            out = sym([mid_inv[i, NM + r, 1] for i in range(6)], [srcs[c][r] for c in range(3)])
-            for c in range(3):
-                errs[c].append(out[c])
-        block_start(srcs + errs, bbase + 1)
+        block_start(srcs, bbase + 1)
         for c in range(3):
             keep_own(mid_src.at[c], srcs[c])
-            keep_own(err.at[0, c], errs[c])
-        block_wait(6, bbase + 1)
-        block_spread([mid_src.at[c] for c in range(3)] + [err.at[0, c] for c in range(3)], bbase + 1)
+        block_wait(3, bbase + 1)
+        block_spread([mid_src.at[c] for c in range(3)], bbase + 1)
+        mid_begin()
         p = 0
         for sweep in range(1, SWEEPS):
             mid_relax(p, sweep)
@@ -655,7 +673,7 @@
             out_specs=pl.BlockSpec(memory_space=pltpu.VMEM),
             scratch_shapes=[
                 vmem(1, NR), vmem(1, NR), vmem(6, NR), vmem(3, NR), vmem(6, NR), vmem(6, NR),
-                vmem(6, WR, 3), vmem(WR, 3), vmem(6, WR, 3), vmem(6, WR, 3), vmem(3, WR, 3),
+                vmem(6, WR, 3), vmem(WR, 3), vmem(WR, 3), vmem(6, WR, 3), vmem(6, WR, 3), vmem(3, WR, 3),
                 vmem(2, 3, WR, 3),
                 vmem(6, GX, GY // 8), vmem(3, GX, GY // 8),
                 pltpu.VMEM((3, GX + 4, GY + 16, 128), f32),

time: 113 us -> 113 us (level)
  no operation moved by 1% of the time
where the time goes in v3:
time: 113 us; the launch traced here: 112 us
  Pallas kernels  109 us (96%)
  local copies, waits for them, and re-layouts  3.05 us (3%)
    pallas_call x1, Pallas kernels, body(): pl.pallas_call(functools.partial(kernel, GX, GY, NR), out_shape=jax.Shape...  109 us
    unnamed x7, local copies, waits for them, and re-layouts  3.05 us

profile of v3, /device:TPU:0, one launch (start us, length us, event | category | flops | bytes accessed | tf_op | source)
XLA Modules:
  0.0 112.5 jit_solution(8465591344838742859)
XLA Ops:
  0.0 0.0 copy-start
  0.0 0.9 copy-done
  0.9 0.0 copy-start.1
  0.9 0.8 copy-done.1
  1.7 0.0 copy-start.2
  1.7 0.8 copy-done.2
  2.4 109.4 %flow_cycles.1 = f32[3,8,8,128]{3,2,1,0:T(8,128)S(1)} custom-call(f32[8,8,128]{2,1,0:T(8,128)S(1)} %copy-done.1, f32[8,8,128]{2,1,0:T(8,128)S(1)} %copy-done.2, f32[3,8,8,128]{3,2,1,0:T(8,128)S(1)} %copy-done), custom_call_target="tpu_custom_call" | custom-call | tf_op jit(solution)/shard_map/flow_cycles/pallas_call | solution.py:669
  111.8 0.6 copy.5
Async XLA Ops:
  0.0 0.9 copy-start
  0.9 0.8 copy-start.1
  1.7 0.8 copy-start.2

commit v4 on v2

--- a/solution.py
+++ b/solution.py
@@ -48,7 +48,7 @@
 
 def kernel(
     GX, GY, NR, first_ref, second_ref, start_ref, flow_ref,
-    mean_ref, weight_ref, tensor_ref, source_ref, face_ref, inv_ref,
+    mean_ref, weight_ref, tensor_ref, source_ref, rest_ref, face_ref, inv_ref,
     mid_t, mid_w, mid_face, mid_inv, mid_src, err,
     coarse_inv, coarse_src, corr,
     xh, yh, xs, ys, bs, br, gs, gb,
@@ -501,16 +501,29 @@
             fine_edges(slot)
         slot = base + 1 + SWEEPS
         fine_start(flow_ref, 3, slot)
+        now = [[flow_ref[c, x] for x in range(NR)] for c in range(3)]
+        for x in range(NR):
+            face = [face_ref[i, x] for i in range(6)]
+            total = functools.reduce(lambda p, q: p + q, face)
+            out = sym([tensor_ref[i, x] for i in range(6)], [now[c][x] for c in range(3)])
+            for c in range(3):
+                v = now[c][x]
+                r = source_ref[c, x] - out[c] - total * v
+                r = r + face[4] * lroll(v, -1) + face[5] * lroll(v, 1)
+                r = r + face[2] * jnp.where(sub < 7, sroll(v, -1), 0.0)
+                r = r + face[3] * jnp.where(sub >= 1, sroll(v, 1), 0.0)
+                if x < NR - 1:
+                    r = r + face[0] * now[c][x + 1]
+                if x > 0:
+                    r = r + face[1] * now[c][x - 1]
+                rest_ref[c, x] = r
         fine_wait(flow_ref, 3, slot)
-        all_rows = [fine_rows(flow_ref, c, slot) for c in range(3)]
-        rest = [[], [], []]
-        for x in range(NR):
-            flows, face = fine_inflow(x, all_rows, slot)
-            total = functools.reduce(lambda p, q: p + q, face)
-            now = [all_rows[c][x + 1] for c in range(3)]
-            out = sym([tensor_ref[i, x] for i in range(6)], now)
-            for c in range(3):
-                rest[c].append(flows[c] - out[c] - total * now[c])
+        for c in range(3):
+            rest_ref[c, 0] = rest_ref[c, 0] + face_ref[1, 0] * xh[slot, 0, c]
+            rest_ref[c, NR - 1] = rest_ref[c, NR - 1] + face_ref[0, NR - 1] * xh[slot, 1, c]
+            for side, y, k in ((0, 0, 3), (1, 7, 2)):
+                rest_ref[c, :, y, :] = rest_ref[c, :, y, :] + face_ref[k, :, y, :] * yh[slot, side, c]
+        rest = [[rest_ref[c, x] for x in range(NR)] for c in range(3)]
         srcs = [restrict_fine(rest[c]) for c in range(3)]
         errs = [[], [], []]
         for r in range(NM):
@@ -654,7 +667,7 @@
             in_specs=[pl.BlockSpec(memory_space=pltpu.VMEM)] * 3,
             out_specs=pl.BlockSpec(memory_space=pltpu.VMEM),
             scratch_shapes=[
-                vmem(1, NR), vmem(1, NR), vmem(6, NR), vmem(3, NR), vmem(6, NR), vmem(6, NR),
+                vmem(1, NR), vmem(1, NR), vmem(6, NR), vmem(3, NR), vmem(3, NR), vmem(6, NR), vmem(6, NR),
                 vmem(6, WR, 3), vmem(WR, 3), vmem(6, WR, 3), vmem(6, WR, 3), vmem(3, WR, 3),
                 vmem(2, 3, WR, 3),
                 vmem(6, GX, GY // 8), vmem(3, GX, GY // 8),

time: 113 us -> 113 us (level)
  no operation moved by 1% of the time
where the time goes in v4:
time: 113 us; the launch traced here: 112 us
  Pallas kernels  109 us (96%)
  local copies, waits for them, and re-layouts  3.05 us (3%)
    pallas_call x1, Pallas kernels, body(): pl.pallas_call(functools.partial(kernel, GX, GY, NR), out_shape=jax.Shape...  109 us
    unnamed x7, local copies, waits for them, and re-layouts  3.05 us

profile of v4, /device:TPU:0, one launch (start us, length us, event | category | flops | bytes accessed | tf_op | source)
XLA Modules:
  0.0 112.3 jit_solution(4694051684440117258)
XLA Ops:
  0.0 0.0 copy-start
  0.0 0.9 copy-done
  0.9 0.0 copy-start.1
  0.9 0.8 copy-done.1
  1.7 0.0 copy-start.2
  1.7 0.8 copy-done.2
  2.4 109.2 %flow_cycles.1 = f32[3,8,8,128]{3,2,1,0:T(8,128)S(1)} custom-call(f32[8,8,128]{2,1,0:T(8,128)S(1)} %copy-done.1, f32[8,8,128]{2,1,0:T(8,128)S(1)} %copy-done.2, f32[3,8,8,128]{3,2,1,0:T(8,128)S(1)} %copy-done), custom_call_target="tpu_custom_call" | custom-call | tf_op jit(solution)/shard_map/flow_cycles/pallas_call | solution.py:664
  111.6 0.6 copy.5
Async XLA Ops:
  0.0 0.9 copy-start
  0.9 0.8 copy-start.1
  1.7 0.8 copy-start.2
